TPU v7x, 256 devices: a whole 4x4x8 slice. The times are simulated.
256 devices in a mesh: tm: 32 (over z, x), elem: 8 (over y, core).
Axes of the slice: x: 4, y: 4, z: 8, core: 2. Of those that a mesh axis runs over, the one named last changes fastest.
Arguments:
- modal_coords: bfloat16 [16384, 512], P('tm'), may hold values from -6 to 6
- stress_modes: bfloat16 [3, 512, 16384], P(None, None, 'elem'), may hold values from -0.375 to 0.375
- step_decay: float32 [16384, 512], P('tm'), may hold values from 0 to 1, as said below
- ply_layup: int32 [128], P('elem'), may hold values from 0 to 15
- lin_table: float32 [16, 2], replicated, may hold values from -0.03 to 0.03
- quad_table: float32 [16, 3], replicated, may hold values from 0.0005 to 0.004
- base_index: float32 [16], replicated, may hold values from 0.9 to 1.1
Outputs:
- column_ks: float32 [16384], P('elem')
- adjoint_states: float32 [16384, 512], P('tm')
Inputs may be any that keep to these rules, and one draw needn't show every extreme that they name: `step_decay`: per-step factors of the modal adjoint states.
All inputs are finite; a program needn't handle non-finite values.
Results may differ from a plain program's by a relative error of at most 0.0027.
Values sent between devices are 32-bit elements; how exact they have to be, the bound alone decides.
A program may use at most 128 MiB of HBM per device.

v0:
```python
import jax
import jax.numpy as jnp
from jax import lax
from jax.sharding import PartitionSpec as P

COL_BLOCK = 128
LAYUPS = 16
sharpness = 100.0


def from_behind(block, axis, distance):
    devices = range(lax.axis_size(axis))
    route = [(i - distance, i) for i in devices if i - distance in devices]
    return lax.ppermute(block, axis, route)


def column_coefs(ply_layup, lin_table, quad_table, base_index):
    levels = jnp.arange(LAYUPS, dtype=jnp.int32)
    onehot = (ply_layup[:, None] == levels[None, :]).astype(jnp.float32)
    coef_table = jnp.concatenate([lin_table, quad_table, base_index[:, None]], axis=1)
    per_block = jnp.dot(onehot, coef_table, precision=lax.Precision.HIGHEST)
    return jnp.repeat(per_block, COL_BLOCK, axis=0).T


def failure_terms(stress, col_coefs):
    stress_one = stress[0]
    stress_two = stress[1]
    stress_shear = stress[2]
    lin_one = col_coefs[0][None, :]
    lin_two = col_coefs[1][None, :]
    quad_one = col_coefs[2][None, :]
    quad_two = col_coefs[3][None, :]
    quad_shear = col_coefs[4][None, :]
    static = col_coefs[5][None, :]
    cross_term = -0.5 * jnp.sqrt(quad_one * quad_two)
    failure_index = (
        static
        + lin_one * stress_one
        + lin_two * stress_two
        + quad_one * stress_one * stress_one
        + quad_two * stress_two * stress_two
        + quad_shear * stress_shear * stress_shear
        + 2.0 * cross_term * stress_one * stress_two
    )
    slopes = (
        lin_one + 2.0 * quad_one * stress_one + 2.0 * cross_term * stress_two,
        lin_two + 2.0 * quad_two * stress_two + 2.0 * cross_term * stress_one,
        2.0 * quad_shear * stress_shear,
    )
    return (failure_index, slopes)


def compose(farther, nearer):
    return (nearer[0] * farther[0], nearer[1] + nearer[0] * farther[1])


def chain_back(decay_rows, load_rows, time_axis):
    carry_scale, offset = lax.associative_scan(
        compose, (decay_rows, load_rows), reverse=True, axis=time_axis
    )
    head_carry = lax.index_in_dim(carry_scale, 0, time_axis, keepdims=False)
    head_offset = lax.index_in_dim(offset, 0, time_axis, keepdims=False)
    incoming = jnp.zeros_like(head_offset)
    for handoff_turn in range(lax.axis_size("tm") - 1):
        incoming = from_behind(head_offset + head_carry * incoming, "tm", -1)
    return offset + carry_scale * jnp.expand_dims(incoming, time_axis)


def body(modal_coords, stress_modes, step_decay, ply_layup, lin_table, quad_table, base_index):
    col_coefs = column_coefs(ply_layup, lin_table, quad_table, base_index)
    stress = jnp.einsum(
        "tm,kmc->ktc", modal_coords, stress_modes, preferred_element_type=jnp.float32
    )
    failure_index, slopes = failure_terms(stress, col_coefs)
    peak_value = lax.pmax(jnp.max(failure_index, axis=0), "tm")
    scaled_exp = jnp.exp(sharpness * (failure_index - peak_value[None, :]))
    mass_total = lax.psum(jnp.sum(scaled_exp, axis=0), "tm")
    column_ks = peak_value + jnp.log(mass_total) / sharpness
    weight = sharpness * scaled_exp / mass_total[None, :]
    sensitivity = jnp.stack([weight * slopes[0], weight * slopes[1], weight * slopes[2]]).astype(
        jnp.bfloat16
    )
    local_loads = lax.dot_general(
        sensitivity, stress_modes, (((0, 2), (0, 2)), ((), ())), preferred_element_type=jnp.float32
    )
    load_rows = lax.psum(local_loads, "elem")
    adjoint = chain_back(step_decay, load_rows, 0)
    return (column_ks, adjoint)


def solution(mesh):
    return jax.shard_map(
        body,
        mesh=mesh,
        in_specs=(P("tm", None), P(None, None, "elem"), P("tm", None), P("elem"), P(), P(), P()),
        out_specs=(P("elem"), P("tm", None)),
        check_vma=False,
    )
```

profile of v0, /device:TPU:128, one launch (start us, length us, event | category | flops | bytes accessed | tf_op | source)
XLA Modules:
  0.0 581.7 jit_solution(983731500119498555)
XLA Ops:
  8.4 5.5 convolution_bitcast_fusion
  13.9 4.3 fusion.46
  18.3 1.5 copy-done.2
  19.7 73.0 %pmax.7 = f32[2048]{0:T(1024)S(1)} all-reduce(f32[2048]{0:T(1024)S(1)} %get-tuple-element.4), channel_id=1, replica_groups=mesh['tm'=32,'elem'=8] {'tm'}, use_global_device_ids=true, to_apply=%region_1.0 | all-reduce | flops 2048 | bytes 16384 | tf_op jit(solution)/shard_map/pmax | solution.py:75
  92.7 2.9 exponential_reduce_fusion
  95.6 70.8 %psum.14 = f32[2048]{0:T(1024)S(1)} all-reduce(f32[2048]{0:T(1024)S(1)} %exponential_reduce_fusion), channel_id=1, replica_groups=mesh['tm'=32,'elem'=8] {'tm'}, use_global_device_ids=true, to_apply=%region_3.0 | all-reduce | flops 2048 | bytes 16384 | tf_op jit(solution)/shard_map/psum | solution.py:77
  166.5 7.8 %multiply_convert_fusion.2 = (bf16[1,512,2048]{2,1,0:T(8,128)(2,1)}, f32[1,512,2048]{2,1,0:T(8,128)S(1)}) fusion(f32[3,512,2048]{2,1,0:T(8,128)} %copy-done.2, f32[2048]{0:T(1024)S(1)} %bitcast.140, f32[2048]{0:T(1024)S(1)} %bitcast.123, f32[2048]{0:T(1024)S(1)} %bitcast.135, f32[2048]{0:T(1024)S(1)} %psum.14, f32[2048]{0:T(1024)S(1)} %pmax.7, ...), kind=kLoop, calls=%fused_computation.34 | loop fusion | flops 27262976 | bytes 18956288 | tf_op jit(solution)/shard_map/convert
  175.4 3.7 multiply_convert_fusion.1
  179.2 7.5 %fusion.21 = f32[512,512]{1,0:T(8,128)} fusion(bf16[3,512,2048]{2,1,0:T(8,128)(2,1)S(1)} %bitcast.58, bf16[1,512,2048]{2,1,0:T(8,128)(2,1)} %get-tuple-element.7, bf16[1,512,2048]{2,1,0:T(8,128)(2,1)} %get-tuple-element.6, bf16[1,512,2048]{2,1,0:T(8,128)(2,1)} %get-tuple-element.2), kind=kOutput, calls=%fused_computation.36 | convolution fusion | flops 3227516928 | bytes 13631488 | tf_op jit(solution)/shard_map/dot_general | solution.py:83
  188.9 2.9 slice.328
  191.9 63.0 %all-reduce.38.cloned.1.call-done = f32[512,512]{1,0:T(8,128)} async-done(((f32[512,512]{1,0:T(8,128)}), f32[512,512]{1,0:T(8,128)}) %all-reduce.38.cloned.1.call-update) | async-done | bytes 1048592 | tf_op jit(solution)/shard_map/psum | solution.py:86
  254.9 3.0 slice.329
  258.2 3.0 slice.333
  267.6 3.7 slice.325
  271.3 4.9 slice.326
  277.0 2.3 add_multiply_fusion
  279.6 4.6 pad.127
  285.0 2.7 pad.126
  288.4 4.5 collective-permute-start
  293.0 1.3 collective-permute-done
  294.3 7.5 %collective-permute-start.1 = (f32[512]{0:T(512)S(1)}, f32[512]{0:T(512)S(1)}, u32[]{:S(2)}, u32[]{:S(2)}) collective-permute-start(f32[512]{0:T(512)S(1)} %multiply_add_fusion.39), channel_id=1, source_target_pairs={{8,0},{16,8},{24,16},{32,24},{40,32},{48,40},{56,48},{64,56},{72,6... | collective-permute-start | bytes 6152 | tf_op jit(solution)/shard_map/ppermute | solution.py:14
  301.8 1.3 collective-permute-done.1
  303.0 7.5 %collective-permute-start.2 = (f32[512]{0:T(512)S(1)}, f32[512]{0:T(512)S(1)}, u32[]{:S(2)}, u32[]{:S(2)}) collective-permute-start(f32[512]{0:T(512)S(1)} %multiply_add_fusion.38), channel_id=1, source_target_pairs={{8,0},{16,8},{24,16},{32,24},{40,32},{48,40},{56,48},{64,56},{72,6... | collective-permute-start | bytes 6152 | tf_op jit(solution)/shard_map/ppermute | solution.py:14
  310.5 1.3 collective-permute-done.2
  311.8 7.5 %collective-permute-start.3 = (f32[512]{0:T(512)S(1)}, f32[512]{0:T(512)S(1)}, u32[]{:S(2)}, u32[]{:S(2)}) collective-permute-start(f32[512]{0:T(512)S(1)} %multiply_add_fusion.37), channel_id=1, source_target_pairs={{8,0},{16,8},{24,16},{32,24},{40,32},{48,40},{56,48},{64,56},{72,6... | collective-permute-start | bytes 6152 | tf_op jit(solution)/shard_map/ppermute | solution.py:14
  319.3 1.3 collective-permute-done.3
  320.6 7.5 %collective-permute-start.4 = (f32[512]{0:T(512)S(1)}, f32[512]{0:T(512)S(1)}, u32[]{:S(2)}, u32[]{:S(2)}) collective-permute-start(f32[512]{0:T(512)S(1)} %multiply_add_fusion.36), channel_id=1, source_target_pairs={{8,0},{16,8},{24,16},{32,24},{40,32},{48,40},{56,48},{64,56},{72,6... | collective-permute-start | bytes 6152 | tf_op jit(solution)/shard_map/ppermute | solution.py:14
  328.1 1.3 collective-permute-done.4
  329.4 7.5 %collective-permute-start.5 = (f32[512]{0:T(512)S(1)}, f32[512]{0:T(512)S(1)}, u32[]{:S(2)}, u32[]{:S(2)}) collective-permute-start(f32[512]{0:T(512)S(1)} %multiply_add_fusion.35), channel_id=1, source_target_pairs={{8,0},{16,8},{24,16},{32,24},{40,32},{48,40},{56,48},{64,56},{72,6... | collective-permute-start | bytes 6152 | tf_op jit(solution)/shard_map/ppermute | solution.py:14
  336.9 1.3 collective-permute-done.5
  338.2 7.5 %collective-permute-start.6 = (f32[512]{0:T(512)S(1)}, f32[512]{0:T(512)S(1)}, u32[]{:S(2)}, u32[]{:S(2)}) collective-permute-start(f32[512]{0:T(512)S(1)} %multiply_add_fusion.34), channel_id=1, source_target_pairs={{8,0},{16,8},{24,16},{32,24},{40,32},{48,40},{56,48},{64,56},{72,6... | collective-permute-start | bytes 6152 | tf_op jit(solution)/shard_map/ppermute | solution.py:14
  345.7 1.3 collective-permute-done.6
  347.0 7.5 %collective-permute-start.7 = (f32[512]{0:T(512)S(1)}, f32[512]{0:T(512)S(1)}, u32[]{:S(2)}, u32[]{:S(2)}) collective-permute-start(f32[512]{0:T(512)S(1)} %multiply_add_fusion.33), channel_id=1, source_target_pairs={{8,0},{16,8},{24,16},{32,24},{40,32},{48,40},{56,48},{64,56},{72,6... | collective-permute-start | bytes 6152 | tf_op jit(solution)/shard_map/ppermute | solution.py:14
  354.5 1.3 collective-permute-done.7
  355.8 7.5 %collective-permute-start.8 = (f32[512]{0:T(512)S(1)}, f32[512]{0:T(512)S(1)}, u32[]{:S(2)}, u32[]{:S(2)}) collective-permute-start(f32[512]{0:T(512)S(1)} %multiply_add_fusion.32), channel_id=1, source_target_pairs={{8,0},{16,8},{24,16},{32,24},{40,32},{48,40},{56,48},{64,56},{72,6... | collective-permute-start | bytes 6152 | tf_op jit(solution)/shard_map/ppermute | solution.py:14
  363.3 1.3 collective-permute-done.8
  364.6 7.5 %collective-permute-start.9 = (f32[512]{0:T(512)S(1)}, f32[512]{0:T(512)S(1)}, u32[]{:S(2)}, u32[]{:S(2)}) collective-permute-start(f32[512]{0:T(512)S(1)} %multiply_add_fusion.31), channel_id=1, source_target_pairs={{8,0},{16,8},{24,16},{32,24},{40,32},{48,40},{56,48},{64,56},{72,6... | collective-permute-start | bytes 6152 | tf_op jit(solution)/shard_map/ppermute | solution.py:14
  373.4 7.5 %collective-permute-start.10 = (f32[512]{0:T(512)S(1)}, f32[512]{0:T(512)S(1)}, u32[]{:S(2)}, u32[]{:S(2)}) collective-permute-start(f32[512]{0:T(512)S(1)} %multiply_add_fusion.30), channel_id=1, source_target_pairs={{8,0},{16,8},{24,16},{32,24},{40,32},{48,40},{56,48},{64,56},{72,6... | collective-permute-start | bytes 6152 | tf_op jit(solution)/shard_map/ppermute | solution.py:14
  382.2 7.5 %collective-permute-start.11 = (f32[512]{0:T(512)S(1)}, f32[512]{0:T(512)S(1)}, u32[]{:S(2)}, u32[]{:S(2)}) collective-permute-start(f32[512]{0:T(512)S(1)} %multiply_add_fusion.29), channel_id=1, source_target_pairs={{8,0},{16,8},{24,16},{32,24},{40,32},{48,40},{56,48},{64,56},{72,6... | collective-permute-start | bytes 6152 | tf_op jit(solution)/shard_map/ppermute | solution.py:14
  391.0 7.5 %collective-permute-start.12 = (f32[512]{0:T(512)S(1)}, f32[512]{0:T(512)S(1)}, u32[]{:S(2)}, u32[]{:S(2)}) collective-permute-start(f32[512]{0:T(512)S(1)} %multiply_add_fusion.28), channel_id=1, source_target_pairs={{8,0},{16,8},{24,16},{32,24},{40,32},{48,40},{56,48},{64,56},{72,6... | collective-permute-start | bytes 6152 | tf_op jit(solution)/shard_map/ppermute | solution.py:14
  399.8 7.5 %collective-permute-start.13 = (f32[512]{0:T(512)S(1)}, f32[512]{0:T(512)S(1)}, u32[]{:S(2)}, u32[]{:S(2)}) collective-permute-start(f32[512]{0:T(512)S(1)} %multiply_add_fusion.27), channel_id=1, source_target_pairs={{8,0},{16,8},{24,16},{32,24},{40,32},{48,40},{56,48},{64,56},{72,6... | collective-permute-start | bytes 6152 | tf_op jit(solution)/shard_map/ppermute | solution.py:14
  407.3 1.3 collective-permute-done.13
  408.6 7.5 %collective-permute-start.14 = (f32[512]{0:T(512)S(1)}, f32[512]{0:T(512)S(1)}, u32[]{:S(2)}, u32[]{:S(2)}) collective-permute-start(f32[512]{0:T(512)S(1)} %multiply_add_fusion.26), channel_id=1, source_target_pairs={{8,0},{16,8},{24,16},{32,24},{40,32},{48,40},{56,48},{64,56},{72,6... | collective-permute-start | bytes 6152 | tf_op jit(solution)/shard_map/ppermute | solution.py:14
  417.3 7.5 %collective-permute-start.15 = (f32[512]{0:T(512)S(1)}, f32[512]{0:T(512)S(1)}, u32[]{:S(2)}, u32[]{:S(2)}) collective-permute-start(f32[512]{0:T(512)S(1)} %multiply_add_fusion.25), channel_id=1, source_target_pairs={{8,0},{16,8},{24,16},{32,24},{40,32},{48,40},{56,48},{64,56},{72,6... | collective-permute-start | bytes 6152 | tf_op jit(solution)/shard_map/ppermute | solution.py:14
  426.1 7.5 %collective-permute-start.16 = (f32[512]{0:T(512)S(1)}, f32[512]{0:T(512)S(1)}, u32[]{:S(2)}, u32[]{:S(2)}) collective-permute-start(f32[512]{0:T(512)S(1)} %multiply_add_fusion.24), channel_id=1, source_target_pairs={{8,0},{16,8},{24,16},{32,24},{40,32},{48,40},{56,48},{64,56},{72,6... | collective-permute-start | bytes 6152 | tf_op jit(solution)/shard_map/ppermute | solution.py:14
  434.9 7.5 %collective-permute-start.17 = (f32[512]{0:T(512)S(1)}, f32[512]{0:T(512)S(1)}, u32[]{:S(2)}, u32[]{:S(2)}) collective-permute-start(f32[512]{0:T(512)S(1)} %multiply_add_fusion.23), channel_id=1, source_target_pairs={{8,0},{16,8},{24,16},{32,24},{40,32},{48,40},{56,48},{64,56},{72,6... | collective-permute-start | bytes 6152 | tf_op jit(solution)/shard_map/ppermute | solution.py:14
  443.7 7.5 %collective-permute-start.18 = (f32[512]{0:T(512)S(1)}, f32[512]{0:T(512)S(1)}, u32[]{:S(2)}, u32[]{:S(2)}) collective-permute-start(f32[512]{0:T(512)S(1)} %multiply_add_fusion.22), channel_id=1, source_target_pairs={{8,0},{16,8},{24,16},{32,24},{40,32},{48,40},{56,48},{64,56},{72,6... | collective-permute-start | bytes 6152 | tf_op jit(solution)/shard_map/ppermute | solution.py:14
  452.5 7.5 %collective-permute-start.19 = (f32[512]{0:T(512)S(1)}, f32[512]{0:T(512)S(1)}, u32[]{:S(2)}, u32[]{:S(2)}) collective-permute-start(f32[512]{0:T(512)S(1)} %multiply_add_fusion.21), channel_id=1, source_target_pairs={{8,0},{16,8},{24,16},{32,24},{40,32},{48,40},{56,48},{64,56},{72,6... | collective-permute-start | bytes 6152 | tf_op jit(solution)/shard_map/ppermute | solution.py:14
  461.3 7.5 %collective-permute-start.20 = (f32[512]{0:T(512)S(1)}, f32[512]{0:T(512)S(1)}, u32[]{:S(2)}, u32[]{:S(2)}) collective-permute-start(f32[512]{0:T(512)S(1)} %multiply_add_fusion.20), channel_id=1, source_target_pairs={{8,0},{16,8},{24,16},{32,24},{40,32},{48,40},{56,48},{64,56},{72,6... | collective-permute-start | bytes 6152 | tf_op jit(solution)/shard_map/ppermute | solution.py:14
  468.8 1.3 collective-permute-done.20
  470.1 7.5 %collective-permute-start.21 = (f32[512]{0:T(512)S(1)}, f32[512]{0:T(512)S(1)}, u32[]{:S(2)}, u32[]{:S(2)}) collective-permute-start(f32[512]{0:T(512)S(1)} %multiply_add_fusion.19), channel_id=1, source_target_pairs={{8,0},{16,8},{24,16},{32,24},{40,32},{48,40},{56,48},{64,56},{72,6... | collective-permute-start | bytes 6152 | tf_op jit(solution)/shard_map/ppermute | solution.py:14
  478.9 7.5 %collective-permute-start.22 = (f32[512]{0:T(512)S(1)}, f32[512]{0:T(512)S(1)}, u32[]{:S(2)}, u32[]{:S(2)}) collective-permute-start(f32[512]{0:T(512)S(1)} %multiply_add_fusion.18), channel_id=1, source_target_pairs={{8,0},{16,8},{24,16},{32,24},{40,32},{48,40},{56,48},{64,56},{72,6... | collective-permute-start | bytes 6152 | tf_op jit(solution)/shard_map/ppermute | solution.py:14
  487.7 7.5 %collective-permute-start.23 = (f32[512]{0:T(512)S(1)}, f32[512]{0:T(512)S(1)}, u32[]{:S(2)}, u32[]{:S(2)}) collective-permute-start(f32[512]{0:T(512)S(1)} %multiply_add_fusion.17), channel_id=1, source_target_pairs={{8,0},{16,8},{24,16},{32,24},{40,32},{48,40},{56,48},{64,56},{72,6... | collective-permute-start | bytes 6152 | tf_op jit(solution)/shard_map/ppermute | solution.py:14
  496.5 7.5 %collective-permute-start.24 = (f32[512]{0:T(512)S(1)}, f32[512]{0:T(512)S(1)}, u32[]{:S(2)}, u32[]{:S(2)}) collective-permute-start(f32[512]{0:T(512)S(1)} %multiply_add_fusion.16), channel_id=1, source_target_pairs={{8,0},{16,8},{24,16},{32,24},{40,32},{48,40},{56,48},{64,56},{72,6... | collective-permute-start | bytes 6152 | tf_op jit(solution)/shard_map/ppermute | solution.py:14
  505.3 7.5 %collective-permute-start.25 = (f32[512]{0:T(512)S(1)}, f32[512]{0:T(512)S(1)}, u32[]{:S(2)}, u32[]{:S(2)}) collective-permute-start(f32[512]{0:T(512)S(1)} %multiply_add_fusion.15), channel_id=1, source_target_pairs={{8,0},{16,8},{24,16},{32,24},{40,32},{48,40},{56,48},{64,56},{72,6... | collective-permute-start | bytes 6152 | tf_op jit(solution)/shard_map/ppermute | solution.py:14
  514.1 7.5 %collective-permute-start.26 = (f32[512]{0:T(512)S(1)}, f32[512]{0:T(512)S(1)}, u32[]{:S(2)}, u32[]{:S(2)}) collective-permute-start(f32[512]{0:T(512)S(1)} %multiply_add_fusion.14), channel_id=1, source_target_pairs={{8,0},{16,8},{24,16},{32,24},{40,32},{48,40},{56,48},{64,56},{72,6... | collective-permute-start | bytes 6152 | tf_op jit(solution)/shard_map/ppermute | solution.py:14
  522.9 7.5 %collective-permute-start.27 = (f32[512]{0:T(512)S(1)}, f32[512]{0:T(512)S(1)}, u32[]{:S(2)}, u32[]{:S(2)}) collective-permute-start(f32[512]{0:T(512)S(1)} %multiply_add_fusion.13), channel_id=1, source_target_pairs={{8,0},{16,8},{24,16},{32,24},{40,32},{48,40},{56,48},{64,56},{72,6... | collective-permute-start | bytes 6152 | tf_op jit(solution)/shard_map/ppermute | solution.py:14
  531.7 7.5 %collective-permute-start.28 = (f32[512]{0:T(512)S(1)}, f32[512]{0:T(512)S(1)}, u32[]{:S(2)}, u32[]{:S(2)}) collective-permute-start(f32[512]{0:T(512)S(1)} %multiply_add_fusion.12), channel_id=1, source_target_pairs={{8,0},{16,8},{24,16},{32,24},{40,32},{48,40},{56,48},{64,56},{72,6... | collective-permute-start | bytes 6152 | tf_op jit(solution)/shard_map/ppermute | solution.py:14
  540.4 7.5 %collective-permute-start.29 = (f32[512]{0:T(512)S(1)}, f32[512]{0:T(512)S(1)}, u32[]{:S(2)}, u32[]{:S(2)}) collective-permute-start(f32[512]{0:T(512)S(1)} %multiply_add_fusion.11), channel_id=1, source_target_pairs={{8,0},{16,8},{24,16},{32,24},{40,32},{48,40},{56,48},{64,56},{72,6... | collective-permute-start | bytes 6152 | tf_op jit(solution)/shard_map/ppermute | solution.py:14
  549.2 7.5 %collective-permute-start.30 = (f32[512]{0:T(512)S(1)}, f32[512]{0:T(512)S(1)}, u32[]{:S(2)}, u32[]{:S(2)}) collective-permute-start(f32[512]{0:T(512)S(1)} %multiply_add_fusion.10), channel_id=1, source_target_pairs={{8,0},{16,8},{24,16},{32,24},{40,32},{48,40},{56,48},{64,56},{72,6... | collective-permute-start | bytes 6152 | tf_op jit(solution)/shard_map/ppermute | solution.py:14
  558.6 1.8 add.404
  560.4 6.9 %rev.9 = f32[512,512]{1,0:T(8,128)S(1)} reverse(f32[512,512]{1,0:T(8,128)} %add.413), dimensions={0} | reverse | bytes 2097152 | tf_op jit(solution)/shard_map/rev | solution.py:58
  567.2 5.2 rev.8
  572.4 2.4 multiply_add_fusion
  (214 shorter events, 39.6 us)
Async XLA Ops:
  7.2 1.2 copy-start
  7.2 247.7 %all-reduce.38.cloned.1.call-start = ((), (), s32[]{:S(2)}) async-start(), calls=%async_computation | async-start | bytes 2097152 | tf_op jit(solution)/shard_map/psum | solution.py:86
  13.9 5.8 copy-start.2
  166.4 9.0 %copy-start.3 = (f32[3,512,2048]{2,1,0:T(8,128)S(1)}, f32[3,512,2048]{2,1,0:T(8,128)}, u32[]{:S(2)}) copy-start(f32[3,512,2048]{2,1,0:T(8,128)} %copy-done.2) | copy-start | bytes 37748740
  166.5 12.7 %slice-start = ((s8[6291456]{0:T(1024)(128)(4,1)}), s8[4194304]{0:T(1024)(128)(4,1)S(1)}, s32[]{:S(2)}) async-start(s8[6291456]{0:T(1024)(128)(4,1)} %bitcast.57), calls=%async_computation.1 | async-start | bytes 8388608
  175.4 3.7 slice-start.1
  179.1 7.5 %copy-start.4 = (f32[512,512]{1,0:T(8,128)S(1)}, f32[512,512]{1,0:T(8,128)}, u32[]{:S(2)}) copy-start(f32[512,512]{1,0:T(8,128)} %param.9) | copy-start | bytes 3145732
  279.4 5.6 copy-start.5
  288.4 5.8 collective-permute-start
  294.3 8.8 %collective-permute-start.1 = (f32[512]{0:T(512)S(1)}, f32[512]{0:T(512)S(1)}, u32[]{:S(2)}, u32[]{:S(2)}) collective-permute-start(f32[512]{0:T(512)S(1)} %multiply_add_fusion.39), channel_id=1, source_target_pairs={{8,0},{16,8},{24,16},{32,24},{40,32},{48,40},{56,48},{64,56},{72,6... | collective-permute-start | bytes 6152 | tf_op jit(solution)/shard_map/ppermute | solution.py:14
  303.0 8.8 %collective-permute-start.2 = (f32[512]{0:T(512)S(1)}, f32[512]{0:T(512)S(1)}, u32[]{:S(2)}, u32[]{:S(2)}) collective-permute-start(f32[512]{0:T(512)S(1)} %multiply_add_fusion.38), channel_id=1, source_target_pairs={{8,0},{16,8},{24,16},{32,24},{40,32},{48,40},{56,48},{64,56},{72,6... | collective-permute-start | bytes 6152 | tf_op jit(solution)/shard_map/ppermute | solution.py:14
  311.8 8.8 %collective-permute-start.3 = (f32[512]{0:T(512)S(1)}, f32[512]{0:T(512)S(1)}, u32[]{:S(2)}, u32[]{:S(2)}) collective-permute-start(f32[512]{0:T(512)S(1)} %multiply_add_fusion.37), channel_id=1, source_target_pairs={{8,0},{16,8},{24,16},{32,24},{40,32},{48,40},{56,48},{64,56},{72,6... | collective-permute-start | bytes 6152 | tf_op jit(solution)/shard_map/ppermute | solution.py:14
  320.6 8.8 %collective-permute-start.4 = (f32[512]{0:T(512)S(1)}, f32[512]{0:T(512)S(1)}, u32[]{:S(2)}, u32[]{:S(2)}) collective-permute-start(f32[512]{0:T(512)S(1)} %multiply_add_fusion.36), channel_id=1, source_target_pairs={{8,0},{16,8},{24,16},{32,24},{40,32},{48,40},{56,48},{64,56},{72,6... | collective-permute-start | bytes 6152 | tf_op jit(solution)/shard_map/ppermute | solution.py:14
  329.4 8.8 %collective-permute-start.5 = (f32[512]{0:T(512)S(1)}, f32[512]{0:T(512)S(1)}, u32[]{:S(2)}, u32[]{:S(2)}) collective-permute-start(f32[512]{0:T(512)S(1)} %multiply_add_fusion.35), channel_id=1, source_target_pairs={{8,0},{16,8},{24,16},{32,24},{40,32},{48,40},{56,48},{64,56},{72,6... | collective-permute-start | bytes 6152 | tf_op jit(solution)/shard_map/ppermute | solution.py:14
  338.2 8.8 %collective-permute-start.6 = (f32[512]{0:T(512)S(1)}, f32[512]{0:T(512)S(1)}, u32[]{:S(2)}, u32[]{:S(2)}) collective-permute-start(f32[512]{0:T(512)S(1)} %multiply_add_fusion.34), channel_id=1, source_target_pairs={{8,0},{16,8},{24,16},{32,24},{40,32},{48,40},{56,48},{64,56},{72,6... | collective-permute-start | bytes 6152 | tf_op jit(solution)/shard_map/ppermute | solution.py:14
  347.0 8.8 %collective-permute-start.7 = (f32[512]{0:T(512)S(1)}, f32[512]{0:T(512)S(1)}, u32[]{:S(2)}, u32[]{:S(2)}) collective-permute-start(f32[512]{0:T(512)S(1)} %multiply_add_fusion.33), channel_id=1, source_target_pairs={{8,0},{16,8},{24,16},{32,24},{40,32},{48,40},{56,48},{64,56},{72,6... | collective-permute-start | bytes 6152 | tf_op jit(solution)/shard_map/ppermute | solution.py:14
  355.8 8.8 %collective-permute-start.8 = (f32[512]{0:T(512)S(1)}, f32[512]{0:T(512)S(1)}, u32[]{:S(2)}, u32[]{:S(2)}) collective-permute-start(f32[512]{0:T(512)S(1)} %multiply_add_fusion.32), channel_id=1, source_target_pairs={{8,0},{16,8},{24,16},{32,24},{40,32},{48,40},{56,48},{64,56},{72,6... | collective-permute-start | bytes 6152 | tf_op jit(solution)/shard_map/ppermute | solution.py:14
  364.6 8.8 %collective-permute-start.9 = (f32[512]{0:T(512)S(1)}, f32[512]{0:T(512)S(1)}, u32[]{:S(2)}, u32[]{:S(2)}) collective-permute-start(f32[512]{0:T(512)S(1)} %multiply_add_fusion.31), channel_id=1, source_target_pairs={{8,0},{16,8},{24,16},{32,24},{40,32},{48,40},{56,48},{64,56},{72,6... | collective-permute-start | bytes 6152 | tf_op jit(solution)/shard_map/ppermute | solution.py:14
  373.4 8.8 %collective-permute-start.10 = (f32[512]{0:T(512)S(1)}, f32[512]{0:T(512)S(1)}, u32[]{:S(2)}, u32[]{:S(2)}) collective-permute-start(f32[512]{0:T(512)S(1)} %multiply_add_fusion.30), channel_id=1, source_target_pairs={{8,0},{16,8},{24,16},{32,24},{40,32},{48,40},{56,48},{64,56},{72,6... | collective-permute-start | bytes 6152 | tf_op jit(solution)/shard_map/ppermute | solution.py:14
  382.2 8.8 %collective-permute-start.11 = (f32[512]{0:T(512)S(1)}, f32[512]{0:T(512)S(1)}, u32[]{:S(2)}, u32[]{:S(2)}) collective-permute-start(f32[512]{0:T(512)S(1)} %multiply_add_fusion.29), channel_id=1, source_target_pairs={{8,0},{16,8},{24,16},{32,24},{40,32},{48,40},{56,48},{64,56},{72,6... | collective-permute-start | bytes 6152 | tf_op jit(solution)/shard_map/ppermute | solution.py:14
  391.0 8.8 %collective-permute-start.12 = (f32[512]{0:T(512)S(1)}, f32[512]{0:T(512)S(1)}, u32[]{:S(2)}, u32[]{:S(2)}) collective-permute-start(f32[512]{0:T(512)S(1)} %multiply_add_fusion.28), channel_id=1, source_target_pairs={{8,0},{16,8},{24,16},{32,24},{40,32},{48,40},{56,48},{64,56},{72,6... | collective-permute-start | bytes 6152 | tf_op jit(solution)/shard_map/ppermute | solution.py:14
  399.8 8.8 %collective-permute-start.13 = (f32[512]{0:T(512)S(1)}, f32[512]{0:T(512)S(1)}, u32[]{:S(2)}, u32[]{:S(2)}) collective-permute-start(f32[512]{0:T(512)S(1)} %multiply_add_fusion.27), channel_id=1, source_target_pairs={{8,0},{16,8},{24,16},{32,24},{40,32},{48,40},{56,48},{64,56},{72,6... | collective-permute-start | bytes 6152 | tf_op jit(solution)/shard_map/ppermute | solution.py:14
  408.6 8.8 %collective-permute-start.14 = (f32[512]{0:T(512)S(1)}, f32[512]{0:T(512)S(1)}, u32[]{:S(2)}, u32[]{:S(2)}) collective-permute-start(f32[512]{0:T(512)S(1)} %multiply_add_fusion.26), channel_id=1, source_target_pairs={{8,0},{16,8},{24,16},{32,24},{40,32},{48,40},{56,48},{64,56},{72,6... | collective-permute-start | bytes 6152 | tf_op jit(solution)/shard_map/ppermute | solution.py:14
  417.3 8.8 %collective-permute-start.15 = (f32[512]{0:T(512)S(1)}, f32[512]{0:T(512)S(1)}, u32[]{:S(2)}, u32[]{:S(2)}) collective-permute-start(f32[512]{0:T(512)S(1)} %multiply_add_fusion.25), channel_id=1, source_target_pairs={{8,0},{16,8},{24,16},{32,24},{40,32},{48,40},{56,48},{64,56},{72,6... | collective-permute-start | bytes 6152 | tf_op jit(solution)/shard_map/ppermute | solution.py:14
  426.1 8.8 %collective-permute-start.16 = (f32[512]{0:T(512)S(1)}, f32[512]{0:T(512)S(1)}, u32[]{:S(2)}, u32[]{:S(2)}) collective-permute-start(f32[512]{0:T(512)S(1)} %multiply_add_fusion.24), channel_id=1, source_target_pairs={{8,0},{16,8},{24,16},{32,24},{40,32},{48,40},{56,48},{64,56},{72,6... | collective-permute-start | bytes 6152 | tf_op jit(solution)/shard_map/ppermute | solution.py:14
  434.9 8.8 %collective-permute-start.17 = (f32[512]{0:T(512)S(1)}, f32[512]{0:T(512)S(1)}, u32[]{:S(2)}, u32[]{:S(2)}) collective-permute-start(f32[512]{0:T(512)S(1)} %multiply_add_fusion.23), channel_id=1, source_target_pairs={{8,0},{16,8},{24,16},{32,24},{40,32},{48,40},{56,48},{64,56},{72,6... | collective-permute-start | bytes 6152 | tf_op jit(solution)/shard_map/ppermute | solution.py:14
  443.7 8.8 %collective-permute-start.18 = (f32[512]{0:T(512)S(1)}, f32[512]{0:T(512)S(1)}, u32[]{:S(2)}, u32[]{:S(2)}) collective-permute-start(f32[512]{0:T(512)S(1)} %multiply_add_fusion.22), channel_id=1, source_target_pairs={{8,0},{16,8},{24,16},{32,24},{40,32},{48,40},{56,48},{64,56},{72,6... | collective-permute-start | bytes 6152 | tf_op jit(solution)/shard_map/ppermute | solution.py:14
  452.5 8.8 %collective-permute-start.19 = (f32[512]{0:T(512)S(1)}, f32[512]{0:T(512)S(1)}, u32[]{:S(2)}, u32[]{:S(2)}) collective-permute-start(f32[512]{0:T(512)S(1)} %multiply_add_fusion.21), channel_id=1, source_target_pairs={{8,0},{16,8},{24,16},{32,24},{40,32},{48,40},{56,48},{64,56},{72,6... | collective-permute-start | bytes 6152 | tf_op jit(solution)/shard_map/ppermute | solution.py:14
  461.3 8.8 %collective-permute-start.20 = (f32[512]{0:T(512)S(1)}, f32[512]{0:T(512)S(1)}, u32[]{:S(2)}, u32[]{:S(2)}) collective-permute-start(f32[512]{0:T(512)S(1)} %multiply_add_fusion.20), channel_id=1, source_target_pairs={{8,0},{16,8},{24,16},{32,24},{40,32},{48,40},{56,48},{64,56},{72,6... | collective-permute-start | bytes 6152 | tf_op jit(solution)/shard_map/ppermute | solution.py:14
  470.1 8.8 %collective-permute-start.21 = (f32[512]{0:T(512)S(1)}, f32[512]{0:T(512)S(1)}, u32[]{:S(2)}, u32[]{:S(2)}) collective-permute-start(f32[512]{0:T(512)S(1)} %multiply_add_fusion.19), channel_id=1, source_target_pairs={{8,0},{16,8},{24,16},{32,24},{40,32},{48,40},{56,48},{64,56},{72,6... | collective-permute-start | bytes 6152 | tf_op jit(solution)/shard_map/ppermute | solution.py:14
  478.9 8.8 %collective-permute-start.22 = (f32[512]{0:T(512)S(1)}, f32[512]{0:T(512)S(1)}, u32[]{:S(2)}, u32[]{:S(2)}) collective-permute-start(f32[512]{0:T(512)S(1)} %multiply_add_fusion.18), channel_id=1, source_target_pairs={{8,0},{16,8},{24,16},{32,24},{40,32},{48,40},{56,48},{64,56},{72,6... | collective-permute-start | bytes 6152 | tf_op jit(solution)/shard_map/ppermute | solution.py:14
  487.7 8.8 %collective-permute-start.23 = (f32[512]{0:T(512)S(1)}, f32[512]{0:T(512)S(1)}, u32[]{:S(2)}, u32[]{:S(2)}) collective-permute-start(f32[512]{0:T(512)S(1)} %multiply_add_fusion.17), channel_id=1, source_target_pairs={{8,0},{16,8},{24,16},{32,24},{40,32},{48,40},{56,48},{64,56},{72,6... | collective-permute-start | bytes 6152 | tf_op jit(solution)/shard_map/ppermute | solution.py:14
  496.5 8.8 %collective-permute-start.24 = (f32[512]{0:T(512)S(1)}, f32[512]{0:T(512)S(1)}, u32[]{:S(2)}, u32[]{:S(2)}) collective-permute-start(f32[512]{0:T(512)S(1)} %multiply_add_fusion.16), channel_id=1, source_target_pairs={{8,0},{16,8},{24,16},{32,24},{40,32},{48,40},{56,48},{64,56},{72,6... | collective-permute-start | bytes 6152 | tf_op jit(solution)/shard_map/ppermute | solution.py:14
  505.3 8.8 %collective-permute-start.25 = (f32[512]{0:T(512)S(1)}, f32[512]{0:T(512)S(1)}, u32[]{:S(2)}, u32[]{:S(2)}) collective-permute-start(f32[512]{0:T(512)S(1)} %multiply_add_fusion.15), channel_id=1, source_target_pairs={{8,0},{16,8},{24,16},{32,24},{40,32},{48,40},{56,48},{64,56},{72,6... | collective-permute-start | bytes 6152 | tf_op jit(solution)/shard_map/ppermute | solution.py:14
  514.1 8.8 %collective-permute-start.26 = (f32[512]{0:T(512)S(1)}, f32[512]{0:T(512)S(1)}, u32[]{:S(2)}, u32[]{:S(2)}) collective-permute-start(f32[512]{0:T(512)S(1)} %multiply_add_fusion.14), channel_id=1, source_target_pairs={{8,0},{16,8},{24,16},{32,24},{40,32},{48,40},{56,48},{64,56},{72,6... | collective-permute-start | bytes 6152 | tf_op jit(solution)/shard_map/ppermute | solution.py:14
  522.9 8.8 %collective-permute-start.27 = (f32[512]{0:T(512)S(1)}, f32[512]{0:T(512)S(1)}, u32[]{:S(2)}, u32[]{:S(2)}) collective-permute-start(f32[512]{0:T(512)S(1)} %multiply_add_fusion.13), channel_id=1, source_target_pairs={{8,0},{16,8},{24,16},{32,24},{40,32},{48,40},{56,48},{64,56},{72,6... | collective-permute-start | bytes 6152 | tf_op jit(solution)/shard_map/ppermute | solution.py:14
  531.7 8.8 %collective-permute-start.28 = (f32[512]{0:T(512)S(1)}, f32[512]{0:T(512)S(1)}, u32[]{:S(2)}, u32[]{:S(2)}) collective-permute-start(f32[512]{0:T(512)S(1)} %multiply_add_fusion.12), channel_id=1, source_target_pairs={{8,0},{16,8},{24,16},{32,24},{40,32},{48,40},{56,48},{64,56},{72,6... | collective-permute-start | bytes 6152 | tf_op jit(solution)/shard_map/ppermute | solution.py:14
  540.4 8.8 %collective-permute-start.29 = (f32[512]{0:T(512)S(1)}, f32[512]{0:T(512)S(1)}, u32[]{:S(2)}, u32[]{:S(2)}) collective-permute-start(f32[512]{0:T(512)S(1)} %multiply_add_fusion.11), channel_id=1, source_target_pairs={{8,0},{16,8},{24,16},{32,24},{40,32},{48,40},{56,48},{64,56},{72,6... | collective-permute-start | bytes 6152 | tf_op jit(solution)/shard_map/ppermute | solution.py:14
  549.2 23.2 %collective-permute-start.30 = (f32[512]{0:T(512)S(1)}, f32[512]{0:T(512)S(1)}, u32[]{:S(2)}, u32[]{:S(2)}) collective-permute-start(f32[512]{0:T(512)S(1)} %multiply_add_fusion.10), channel_id=1, source_target_pairs={{8,0},{16,8},{24,16},{32,24},{40,32},{48,40},{56,48},{64,56},{72,6... | collective-permute-start | bytes 6152 | tf_op jit(solution)/shard_map/ppermute | solution.py:14
  558.6 16.3 %copy-start.1 = (bf16[512,512]{1,0:T(8,128)(2,1)S(1)}, bf16[512,512]{1,0:T(8,128)(2,1)}, u32[]{:S(2)}) copy-start(bf16[512,512]{1,0:T(8,128)(2,1)} %param.7) | copy-start | bytes 1572868
Sparse Core Ops, SparseCore 0:
  186.8 68.0 all-reduce.37
where the time goes:
time: 588 us; the launch traced here: 582 us
  starting transfers between devices  229 us (39%)
  blocking collectives  144 us (24%)
  waiting for transfers between devices  102 us (17%)
  local copies, waits for them, and re-layouts  47.5 us (8%)
  other arithmetic  30.2 us (5%)
  between operations  15.2 us (3%)
  matrix products  14 us (2%)
    ppermute x31, starting transfers between devices, from_behind(): return lax.ppermute(block, axis, route)  229 us
    pmax x1, blocking collectives, body(): peak_value = lax.pmax(jnp.max(failure_index, axis=0), 'tm')  73 us
    psum x1, blocking collectives, body(): mass_total = lax.psum(jnp.sum(scaled_exp, axis=0), 'tm')  70.8 us
    psum x1, waiting for transfers between devices, body(): load_rows = lax.psum(local_loads, 'elem')  63 us
    ppermute x31, waiting for transfers between devices, from_behind(): return lax.ppermute(block, axis, route)  38.6 us
    slice x66, local copies, waits for them, and re-layouts, chain_back(): lax.associative_scan(compose, (decay_rows, load_rows), reverse=True, axis...  24.4 us
    rev x2, local copies, waits for them, and re-layouts, chain_back(): lax.associative_scan(compose, (decay_rows, load_rows), reverse=True, axis...  12 us
  transfers between devices with their start and end apart: 32, of which 31 were waited for; matrix products, arithmetic and copies ran while one was open for 4% of the time, Pallas kernels for 0%

commit v1 on v0

--- a/solution.py
+++ b/solution.py
@@ -74,7 +74,7 @@
     failure_index, slopes = failure_terms(stress, col_coefs)
     peak_value = lax.pmax(jnp.max(failure_index, axis=0), "tm")
     scaled_exp = jnp.exp(sharpness * (failure_index - peak_value[None, :]))
-    mass_total = lax.psum(jnp.sum(scaled_exp, axis=0), "tm")
+    mass_total = jnp.sum(lax.all_gather(jnp.sum(scaled_exp, axis=0), "tm"), axis=0)
     column_ks = peak_value + jnp.log(mass_total) / sharpness
     weight = sharpness * scaled_exp / mass_total[None, :]
     sensitivity = jnp.stack([weight * slopes[0], weight * slopes[1], weight * slopes[2]]).astype(

time: 588 us -> 564 us (0.959)
  blocking collectives: 144 us -> 119 us
    psum x1 -> x0, blocking collectives: 70.8 us -> none  [body(): mass_total = lax.psum(jnp.sum(scaled_exp, axis=0), 'tm')]
    all_gather x0 -> x1, blocking collectives: none -> 45.8 us  [body(): lax.all_gather(jnp.sum(scaled_exp, axis=0), 'tm')]
where the time goes in v1:
time: 564 us; the launch traced here: 558 us
  starting transfers between devices  230 us (41%)
  blocking collectives  119 us (21%)
  waiting for transfers between devices  103 us (18%)
  local copies, waits for them, and re-layouts  47.3 us (8%)
  other arithmetic  30.5 us (5%)
  between operations  15.2 us (3%)
  matrix products  14 us (2%)
    ppermute x31, starting transfers between devices, from_behind(): return lax.ppermute(block, axis, route)  230 us
    pmax x1, blocking collectives, body(): peak_value = lax.pmax(jnp.max(failure_index, axis=0), 'tm')  73 us
    psum x1, waiting for transfers between devices, body(): load_rows = lax.psum(local_loads, 'elem')  64.3 us
    all_gather x1, blocking collectives, body(): lax.all_gather(jnp.sum(scaled_exp, axis=0), 'tm')  45.8 us
    ppermute x31, waiting for transfers between devices, from_behind(): return lax.ppermute(block, axis, route)  38.4 us
    slice x66, local copies, waits for them, and re-layouts, chain_back(): lax.associative_scan(compose, (decay_rows, load_rows), reverse=True, axis...  24.4 us
    rev x2, local copies, waits for them, and re-layouts, chain_back(): lax.associative_scan(compose, (decay_rows, load_rows), reverse=True, axis...  12 us
    another operation x2, other arithmetic  11.7 us
  transfers between devices with their start and end apart: 32, of which 31 were waited for; matrix products, arithmetic and copies ran while one was open for 4% of the time, Pallas kernels for 0%

profile of v1, /device:TPU:128, one launch (start us, length us, event | category | flops | bytes accessed | tf_op | source)
XLA Modules:
  0.0 558.1 jit_solution(3512406175308989790)
XLA Ops:
  8.4 5.5 convolution_bitcast_fusion
  13.9 4.3 fusion.46
  18.3 1.5 copy-done.2
  19.7 73.0 %pmax.7 = f32[2048]{0:T(1024)S(1)} all-reduce(f32[2048]{0:T(1024)S(1)} %get-tuple-element.4), channel_id=1, replica_groups=mesh['tm'=32,'elem'=8] {'tm'}, use_global_device_ids=true, to_apply=%region_1.0 | all-reduce | flops 2048 | bytes 16384 | tf_op jit(solution)/shard_map/pmax | solution.py:75
  92.7 2.9 exponential_reduce_fusion
  95.6 45.8 %all-gather = f32[65536]{0:T(1024)S(1)} all-gather(f32[2048]{0:T(1024)S(1)} %exponential_reduce_fusion), channel_id=2, replica_groups=mesh['tm'=32,'elem'=8] {'tm'}, dimensions={0}, use_global_device_ids=true | all-gather | bytes 270336 | tf_op jit(solution)/shard_map/all_gather | solution.py:77
  141.6 8.0 %multiply_convert_fusion.2 = (bf16[1,512,2048]{2,1,0:T(8,128)(2,1)}, f32[1,512,2048]{2,1,0:T(8,128)S(1)}) fusion(f32[3,512,2048]{2,1,0:T(8,128)} %copy-done.2, f32[2048]{0:T(1024)S(1)} %bitcast.140, f32[2048]{0:T(1024)S(1)} %bitcast.123, f32[2048]{0:T(1024)S(1)} %bitcast.135, f32[2048]{0:T(1024)S(1)} %reduce_sum.19, f32[2048]{0:T(1024)S(1)} %pmax.7, ...), kind=kLoop, calls=%fused_computation.34 | loop fusion | flops 27262976 | bytes 18956288 | tf_op jit(solution)/shard_map/convert
  150.5 3.7 multiply_convert_fusion.1
  154.2 7.5 %fusion.21 = f32[512,512]{1,0:T(8,128)} fusion(bf16[3,512,2048]{2,1,0:T(8,128)(2,1)S(1)} %bitcast.58, bf16[1,512,2048]{2,1,0:T(8,128)(2,1)} %get-tuple-element.7, bf16[1,512,2048]{2,1,0:T(8,128)(2,1)} %get-tuple-element.6, bf16[1,512,2048]{2,1,0:T(8,128)(2,1)} %get-tuple-element.2), kind=kOutput, calls=%fused_computation.36 | convolution fusion | flops 3227516928 | bytes 13631488 | tf_op jit(solution)/shard_map/dot_general | solution.py:83
  164.0 2.9 slice.328
  166.9 64.3 %all-reduce.38.cloned.1.call-done = f32[512,512]{1,0:T(8,128)} async-done(((f32[512,512]{1,0:T(8,128)}), f32[512,512]{1,0:T(8,128)}) %all-reduce.38.cloned.1.call-update) | async-done | bytes 1048592 | tf_op jit(solution)/shard_map/psum | solution.py:86
  231.2 3.0 slice.329
  234.5 3.0 slice.333
  244.0 3.7 slice.325
  247.6 4.9 slice.326
  253.4 2.3 add_multiply_fusion
  255.9 4.6 pad.127
  261.4 2.7 pad.126
  264.8 4.5 collective-permute-start
  269.3 1.3 collective-permute-done
  270.6 7.5 %collective-permute-start.1 = (f32[512]{0:T(512)S(1)}, f32[512]{0:T(512)S(1)}, u32[]{:S(2)}, u32[]{:S(2)}) collective-permute-start(f32[512]{0:T(512)S(1)} %multiply_add_fusion.39), channel_id=1, source_target_pairs={{8,0},{16,8},{24,16},{32,24},{40,32},{48,40},{56,48},{64,56},{72,6... | collective-permute-start | bytes 6152 | tf_op jit(solution)/shard_map/ppermute | solution.py:14
  278.1 1.3 collective-permute-done.1
  279.4 7.5 %collective-permute-start.2 = (f32[512]{0:T(512)S(1)}, f32[512]{0:T(512)S(1)}, u32[]{:S(2)}, u32[]{:S(2)}) collective-permute-start(f32[512]{0:T(512)S(1)} %multiply_add_fusion.38), channel_id=1, source_target_pairs={{8,0},{16,8},{24,16},{32,24},{40,32},{48,40},{56,48},{64,56},{72,6... | collective-permute-start | bytes 6152 | tf_op jit(solution)/shard_map/ppermute | solution.py:14
  286.9 1.3 collective-permute-done.2
  288.2 7.5 %collective-permute-start.3 = (f32[512]{0:T(512)S(1)}, f32[512]{0:T(512)S(1)}, u32[]{:S(2)}, u32[]{:S(2)}) collective-permute-start(f32[512]{0:T(512)S(1)} %multiply_add_fusion.37), channel_id=1, source_target_pairs={{8,0},{16,8},{24,16},{32,24},{40,32},{48,40},{56,48},{64,56},{72,6... | collective-permute-start | bytes 6152 | tf_op jit(solution)/shard_map/ppermute | solution.py:14
  295.7 1.3 collective-permute-done.3
  297.0 7.5 %collective-permute-start.4 = (f32[512]{0:T(512)S(1)}, f32[512]{0:T(512)S(1)}, u32[]{:S(2)}, u32[]{:S(2)}) collective-permute-start(f32[512]{0:T(512)S(1)} %multiply_add_fusion.36), channel_id=1, source_target_pairs={{8,0},{16,8},{24,16},{32,24},{40,32},{48,40},{56,48},{64,56},{72,6... | collective-permute-start | bytes 6152 | tf_op jit(solution)/shard_map/ppermute | solution.py:14
  304.5 1.3 collective-permute-done.4
  305.8 7.7 %collective-permute-start.5 = (f32[512]{0:T(512)S(1)}, f32[512]{0:T(512)S(1)}, u32[]{:S(2)}, u32[]{:S(2)}) collective-permute-start(f32[512]{0:T(512)S(1)} %multiply_add_fusion.35), channel_id=1, source_target_pairs={{8,0},{16,8},{24,16},{32,24},{40,32},{48,40},{56,48},{64,56},{72,6... | collective-permute-start | bytes 6152 | tf_op jit(solution)/shard_map/ppermute | solution.py:14
  314.6 7.5 %collective-permute-start.6 = (f32[512]{0:T(512)S(1)}, f32[512]{0:T(512)S(1)}, u32[]{:S(2)}, u32[]{:S(2)}) collective-permute-start(f32[512]{0:T(512)S(1)} %multiply_add_fusion.34), channel_id=1, source_target_pairs={{8,0},{16,8},{24,16},{32,24},{40,32},{48,40},{56,48},{64,56},{72,6... | collective-permute-start | bytes 6152 | tf_op jit(solution)/shard_map/ppermute | solution.py:14
  322.1 1.3 collective-permute-done.6
  323.4 7.5 %collective-permute-start.7 = (f32[512]{0:T(512)S(1)}, f32[512]{0:T(512)S(1)}, u32[]{:S(2)}, u32[]{:S(2)}) collective-permute-start(f32[512]{0:T(512)S(1)} %multiply_add_fusion.33), channel_id=1, source_target_pairs={{8,0},{16,8},{24,16},{32,24},{40,32},{48,40},{56,48},{64,56},{72,6... | collective-permute-start | bytes 6152 | tf_op jit(solution)/shard_map/ppermute | solution.py:14
  330.9 1.3 collective-permute-done.7
  332.2 7.5 %collective-permute-start.8 = (f32[512]{0:T(512)S(1)}, f32[512]{0:T(512)S(1)}, u32[]{:S(2)}, u32[]{:S(2)}) collective-permute-start(f32[512]{0:T(512)S(1)} %multiply_add_fusion.32), channel_id=1, source_target_pairs={{8,0},{16,8},{24,16},{32,24},{40,32},{48,40},{56,48},{64,56},{72,6... | collective-permute-start | bytes 6152 | tf_op jit(solution)/shard_map/ppermute | solution.py:14
  339.7 1.3 collective-permute-done.8
  341.0 7.5 %collective-permute-start.9 = (f32[512]{0:T(512)S(1)}, f32[512]{0:T(512)S(1)}, u32[]{:S(2)}, u32[]{:S(2)}) collective-permute-start(f32[512]{0:T(512)S(1)} %multiply_add_fusion.31), channel_id=1, source_target_pairs={{8,0},{16,8},{24,16},{32,24},{40,32},{48,40},{56,48},{64,56},{72,6... | collective-permute-start | bytes 6152 | tf_op jit(solution)/shard_map/ppermute | solution.py:14
  348.5 1.3 collective-permute-done.9
  349.8 7.5 %collective-permute-start.10 = (f32[512]{0:T(512)S(1)}, f32[512]{0:T(512)S(1)}, u32[]{:S(2)}, u32[]{:S(2)}) collective-permute-start(f32[512]{0:T(512)S(1)} %multiply_add_fusion.30), channel_id=1, source_target_pairs={{8,0},{16,8},{24,16},{32,24},{40,32},{48,40},{56,48},{64,56},{72,6... | collective-permute-start | bytes 6152 | tf_op jit(solution)/shard_map/ppermute | solution.py:14
  358.5 7.5 %collective-permute-start.11 = (f32[512]{0:T(512)S(1)}, f32[512]{0:T(512)S(1)}, u32[]{:S(2)}, u32[]{:S(2)}) collective-permute-start(f32[512]{0:T(512)S(1)} %multiply_add_fusion.29), channel_id=1, source_target_pairs={{8,0},{16,8},{24,16},{32,24},{40,32},{48,40},{56,48},{64,56},{72,6... | collective-permute-start | bytes 6152 | tf_op jit(solution)/shard_map/ppermute | solution.py:14
  367.3 7.5 %collective-permute-start.12 = (f32[512]{0:T(512)S(1)}, f32[512]{0:T(512)S(1)}, u32[]{:S(2)}, u32[]{:S(2)}) collective-permute-start(f32[512]{0:T(512)S(1)} %multiply_add_fusion.28), channel_id=1, source_target_pairs={{8,0},{16,8},{24,16},{32,24},{40,32},{48,40},{56,48},{64,56},{72,6... | collective-permute-start | bytes 6152 | tf_op jit(solution)/shard_map/ppermute | solution.py:14
  376.1 7.5 %collective-permute-start.13 = (f32[512]{0:T(512)S(1)}, f32[512]{0:T(512)S(1)}, u32[]{:S(2)}, u32[]{:S(2)}) collective-permute-start(f32[512]{0:T(512)S(1)} %multiply_add_fusion.27), channel_id=1, source_target_pairs={{8,0},{16,8},{24,16},{32,24},{40,32},{48,40},{56,48},{64,56},{72,6... | collective-permute-start | bytes 6152 | tf_op jit(solution)/shard_map/ppermute | solution.py:14
  384.9 7.5 %collective-permute-start.14 = (f32[512]{0:T(512)S(1)}, f32[512]{0:T(512)S(1)}, u32[]{:S(2)}, u32[]{:S(2)}) collective-permute-start(f32[512]{0:T(512)S(1)} %multiply_add_fusion.26), channel_id=1, source_target_pairs={{8,0},{16,8},{24,16},{32,24},{40,32},{48,40},{56,48},{64,56},{72,6... | collective-permute-start | bytes 6152 | tf_op jit(solution)/shard_map/ppermute | solution.py:14
  392.4 1.3 collective-permute-done.14
  393.7 7.5 %collective-permute-start.15 = (f32[512]{0:T(512)S(1)}, f32[512]{0:T(512)S(1)}, u32[]{:S(2)}, u32[]{:S(2)}) collective-permute-start(f32[512]{0:T(512)S(1)} %multiply_add_fusion.25), channel_id=1, source_target_pairs={{8,0},{16,8},{24,16},{32,24},{40,32},{48,40},{56,48},{64,56},{72,6... | collective-permute-start | bytes 6152 | tf_op jit(solution)/shard_map/ppermute | solution.py:14
  402.5 7.5 %collective-permute-start.16 = (f32[512]{0:T(512)S(1)}, f32[512]{0:T(512)S(1)}, u32[]{:S(2)}, u32[]{:S(2)}) collective-permute-start(f32[512]{0:T(512)S(1)} %multiply_add_fusion.24), channel_id=1, source_target_pairs={{8,0},{16,8},{24,16},{32,24},{40,32},{48,40},{56,48},{64,56},{72,6... | collective-permute-start | bytes 6152 | tf_op jit(solution)/shard_map/ppermute | solution.py:14
  411.3 7.5 %collective-permute-start.17 = (f32[512]{0:T(512)S(1)}, f32[512]{0:T(512)S(1)}, u32[]{:S(2)}, u32[]{:S(2)}) collective-permute-start(f32[512]{0:T(512)S(1)} %multiply_add_fusion.23), channel_id=1, source_target_pairs={{8,0},{16,8},{24,16},{32,24},{40,32},{48,40},{56,48},{64,56},{72,6... | collective-permute-start | bytes 6152 | tf_op jit(solution)/shard_map/ppermute | solution.py:14
  420.1 7.5 %collective-permute-start.18 = (f32[512]{0:T(512)S(1)}, f32[512]{0:T(512)S(1)}, u32[]{:S(2)}, u32[]{:S(2)}) collective-permute-start(f32[512]{0:T(512)S(1)} %multiply_add_fusion.22), channel_id=1, source_target_pairs={{8,0},{16,8},{24,16},{32,24},{40,32},{48,40},{56,48},{64,56},{72,6... | collective-permute-start | bytes 6152 | tf_op jit(solution)/shard_map/ppermute | solution.py:14
  428.9 7.5 %collective-permute-start.19 = (f32[512]{0:T(512)S(1)}, f32[512]{0:T(512)S(1)}, u32[]{:S(2)}, u32[]{:S(2)}) collective-permute-start(f32[512]{0:T(512)S(1)} %multiply_add_fusion.21), channel_id=1, source_target_pairs={{8,0},{16,8},{24,16},{32,24},{40,32},{48,40},{56,48},{64,56},{72,6... | collective-permute-start | bytes 6152 | tf_op jit(solution)/shard_map/ppermute | solution.py:14
  437.7 7.5 %collective-permute-start.20 = (f32[512]{0:T(512)S(1)}, f32[512]{0:T(512)S(1)}, u32[]{:S(2)}, u32[]{:S(2)}) collective-permute-start(f32[512]{0:T(512)S(1)} %multiply_add_fusion.20), channel_id=1, source_target_pairs={{8,0},{16,8},{24,16},{32,24},{40,32},{48,40},{56,48},{64,56},{72,6... | collective-permute-start | bytes 6152 | tf_op jit(solution)/shard_map/ppermute | solution.py:14
  446.5 7.5 %collective-permute-start.21 = (f32[512]{0:T(512)S(1)}, f32[512]{0:T(512)S(1)}, u32[]{:S(2)}, u32[]{:S(2)}) collective-permute-start(f32[512]{0:T(512)S(1)} %multiply_add_fusion.19), channel_id=1, source_target_pairs={{8,0},{16,8},{24,16},{32,24},{40,32},{48,40},{56,48},{64,56},{72,6... | collective-permute-start | bytes 6152 | tf_op jit(solution)/shard_map/ppermute | solution.py:14
  454.0 1.3 collective-permute-done.21
  455.3 7.5 %collective-permute-start.22 = (f32[512]{0:T(512)S(1)}, f32[512]{0:T(512)S(1)}, u32[]{:S(2)}, u32[]{:S(2)}) collective-permute-start(f32[512]{0:T(512)S(1)} %multiply_add_fusion.18), channel_id=1, source_target_pairs={{8,0},{16,8},{24,16},{32,24},{40,32},{48,40},{56,48},{64,56},{72,6... | collective-permute-start | bytes 6152 | tf_op jit(solution)/shard_map/ppermute | solution.py:14
  464.1 7.5 %collective-permute-start.23 = (f32[512]{0:T(512)S(1)}, f32[512]{0:T(512)S(1)}, u32[]{:S(2)}, u32[]{:S(2)}) collective-permute-start(f32[512]{0:T(512)S(1)} %multiply_add_fusion.17), channel_id=1, source_target_pairs={{8,0},{16,8},{24,16},{32,24},{40,32},{48,40},{56,48},{64,56},{72,6... | collective-permute-start | bytes 6152 | tf_op jit(solution)/shard_map/ppermute | solution.py:14
  472.8 7.5 %collective-permute-start.24 = (f32[512]{0:T(512)S(1)}, f32[512]{0:T(512)S(1)}, u32[]{:S(2)}, u32[]{:S(2)}) collective-permute-start(f32[512]{0:T(512)S(1)} %multiply_add_fusion.16), channel_id=1, source_target_pairs={{8,0},{16,8},{24,16},{32,24},{40,32},{48,40},{56,48},{64,56},{72,6... | collective-permute-start | bytes 6152 | tf_op jit(solution)/shard_map/ppermute | solution.py:14
  481.6 7.5 %collective-permute-start.25 = (f32[512]{0:T(512)S(1)}, f32[512]{0:T(512)S(1)}, u32[]{:S(2)}, u32[]{:S(2)}) collective-permute-start(f32[512]{0:T(512)S(1)} %multiply_add_fusion.15), channel_id=1, source_target_pairs={{8,0},{16,8},{24,16},{32,24},{40,32},{48,40},{56,48},{64,56},{72,6... | collective-permute-start | bytes 6152 | tf_op jit(solution)/shard_map/ppermute | solution.py:14
  490.4 7.5 %collective-permute-start.26 = (f32[512]{0:T(512)S(1)}, f32[512]{0:T(512)S(1)}, u32[]{:S(2)}, u32[]{:S(2)}) collective-permute-start(f32[512]{0:T(512)S(1)} %multiply_add_fusion.14), channel_id=1, source_target_pairs={{8,0},{16,8},{24,16},{32,24},{40,32},{48,40},{56,48},{64,56},{72,6... | collective-permute-start | bytes 6152 | tf_op jit(solution)/shard_map/ppermute | solution.py:14
  499.2 7.5 %collective-permute-start.27 = (f32[512]{0:T(512)S(1)}, f32[512]{0:T(512)S(1)}, u32[]{:S(2)}, u32[]{:S(2)}) collective-permute-start(f32[512]{0:T(512)S(1)} %multiply_add_fusion.13), channel_id=1, source_target_pairs={{8,0},{16,8},{24,16},{32,24},{40,32},{48,40},{56,48},{64,56},{72,6... | collective-permute-start | bytes 6152 | tf_op jit(solution)/shard_map/ppermute | solution.py:14
  508.0 7.5 %collective-permute-start.28 = (f32[512]{0:T(512)S(1)}, f32[512]{0:T(512)S(1)}, u32[]{:S(2)}, u32[]{:S(2)}) collective-permute-start(f32[512]{0:T(512)S(1)} %multiply_add_fusion.12), channel_id=1, source_target_pairs={{8,0},{16,8},{24,16},{32,24},{40,32},{48,40},{56,48},{64,56},{72,6... | collective-permute-start | bytes 6152 | tf_op jit(solution)/shard_map/ppermute | solution.py:14
  516.8 7.5 %collective-permute-start.29 = (f32[512]{0:T(512)S(1)}, f32[512]{0:T(512)S(1)}, u32[]{:S(2)}, u32[]{:S(2)}) collective-permute-start(f32[512]{0:T(512)S(1)} %multiply_add_fusion.11), channel_id=1, source_target_pairs={{8,0},{16,8},{24,16},{32,24},{40,32},{48,40},{56,48},{64,56},{72,6... | collective-permute-start | bytes 6152 | tf_op jit(solution)/shard_map/ppermute | solution.py:14
  525.6 7.5 %collective-permute-start.30 = (f32[512]{0:T(512)S(1)}, f32[512]{0:T(512)S(1)}, u32[]{:S(2)}, u32[]{:S(2)}) collective-permute-start(f32[512]{0:T(512)S(1)} %multiply_add_fusion.10), channel_id=1, source_target_pairs={{8,0},{16,8},{24,16},{32,24},{40,32},{48,40},{56,48},{64,56},{72,6... | collective-permute-start | bytes 6152 | tf_op jit(solution)/shard_map/ppermute | solution.py:14
  534.9 1.8 add.402
  536.7 6.9 %rev.9 = f32[512,512]{1,0:T(8,128)S(1)} reverse(f32[512,512]{1,0:T(8,128)} %add.411), dimensions={0} | reverse | bytes 2097152 | tf_op jit(solution)/shard_map/rev | solution.py:58
  543.6 5.2 rev.8
  548.8 2.4 multiply_add_fusion
  (216 shorter events, 39.2 us)
Async XLA Ops:
  7.2 1.2 copy-start
  7.2 224.1 %all-reduce.38.cloned.1.call-start = ((), (), s32[]{:S(2)}) async-start(), calls=%async_computation | async-start | bytes 2097152 | tf_op jit(solution)/shard_map/psum | solution.py:86
  13.9 5.8 %copy-start.2 = (f32[3,512,2048]{2,1,0:T(8,128)}, f32[3,512,2048]{2,1,0:T(8,128)S(1)}, u32[]{:S(2)}) copy-start(f32[3,512,2048]{2,1,0:T(8,128)S(1)} %convolution_bitcast_fusion) | copy-start | bytes 37748740
  141.5 9.0 %copy-start.3 = (f32[3,512,2048]{2,1,0:T(8,128)S(1)}, f32[3,512,2048]{2,1,0:T(8,128)}, u32[]{:S(2)}) copy-start(f32[3,512,2048]{2,1,0:T(8,128)} %copy-done.2) | copy-start | bytes 37748740
  141.5 12.7 %slice-start = ((s8[6291456]{0:T(1024)(128)(4,1)}), s8[4194304]{0:T(1024)(128)(4,1)S(1)}, s32[]{:S(2)}) async-start(s8[6291456]{0:T(1024)(128)(4,1)} %bitcast.57), calls=%async_computation.1 | async-start | bytes 8388608
  150.5 3.7 slice-start.1
  154.2 7.5 %copy-start.4 = (f32[512,512]{1,0:T(8,128)S(1)}, f32[512,512]{1,0:T(8,128)}, u32[]{:S(2)}) copy-start(f32[512,512]{1,0:T(8,128)} %param.9) | copy-start | bytes 3145732
  255.7 5.6 copy-start.5
  264.8 5.8 %collective-permute-start = (f32[512]{0:T(512)S(1)}, f32[512]{0:T(512)S(1)}, u32[]{:S(2)}, u32[]{:S(2)}) collective-permute-start(f32[512]{0:T(512)S(1)} %multiply_add_fusion.40), channel_id=1, source_target_pairs={{8,0},{16,8},{24,16},{32,24},{40,32},{48,40},{56,48},{64,56},{72,6... | collective-permute-start | bytes 6152 | tf_op jit(solution)/shard_map/ppermute | solution.py:14
  270.6 8.8 %collective-permute-start.1 = (f32[512]{0:T(512)S(1)}, f32[512]{0:T(512)S(1)}, u32[]{:S(2)}, u32[]{:S(2)}) collective-permute-start(f32[512]{0:T(512)S(1)} %multiply_add_fusion.39), channel_id=1, source_target_pairs={{8,0},{16,8},{24,16},{32,24},{40,32},{48,40},{56,48},{64,56},{72,6... | collective-permute-start | bytes 6152 | tf_op jit(solution)/shard_map/ppermute | solution.py:14
  279.4 8.8 %collective-permute-start.2 = (f32[512]{0:T(512)S(1)}, f32[512]{0:T(512)S(1)}, u32[]{:S(2)}, u32[]{:S(2)}) collective-permute-start(f32[512]{0:T(512)S(1)} %multiply_add_fusion.38), channel_id=1, source_target_pairs={{8,0},{16,8},{24,16},{32,24},{40,32},{48,40},{56,48},{64,56},{72,6... | collective-permute-start | bytes 6152 | tf_op jit(solution)/shard_map/ppermute | solution.py:14
  288.2 8.8 %collective-permute-start.3 = (f32[512]{0:T(512)S(1)}, f32[512]{0:T(512)S(1)}, u32[]{:S(2)}, u32[]{:S(2)}) collective-permute-start(f32[512]{0:T(512)S(1)} %multiply_add_fusion.37), channel_id=1, source_target_pairs={{8,0},{16,8},{24,16},{32,24},{40,32},{48,40},{56,48},{64,56},{72,6... | collective-permute-start | bytes 6152 | tf_op jit(solution)/shard_map/ppermute | solution.py:14
  297.0 8.8 %collective-permute-start.4 = (f32[512]{0:T(512)S(1)}, f32[512]{0:T(512)S(1)}, u32[]{:S(2)}, u32[]{:S(2)}) collective-permute-start(f32[512]{0:T(512)S(1)} %multiply_add_fusion.36), channel_id=1, source_target_pairs={{8,0},{16,8},{24,16},{32,24},{40,32},{48,40},{56,48},{64,56},{72,6... | collective-permute-start | bytes 6152 | tf_op jit(solution)/shard_map/ppermute | solution.py:14
  305.8 8.8 %collective-permute-start.5 = (f32[512]{0:T(512)S(1)}, f32[512]{0:T(512)S(1)}, u32[]{:S(2)}, u32[]{:S(2)}) collective-permute-start(f32[512]{0:T(512)S(1)} %multiply_add_fusion.35), channel_id=1, source_target_pairs={{8,0},{16,8},{24,16},{32,24},{40,32},{48,40},{56,48},{64,56},{72,6... | collective-permute-start | bytes 6152 | tf_op jit(solution)/shard_map/ppermute | solution.py:14
  314.6 8.8 %collective-permute-start.6 = (f32[512]{0:T(512)S(1)}, f32[512]{0:T(512)S(1)}, u32[]{:S(2)}, u32[]{:S(2)}) collective-permute-start(f32[512]{0:T(512)S(1)} %multiply_add_fusion.34), channel_id=1, source_target_pairs={{8,0},{16,8},{24,16},{32,24},{40,32},{48,40},{56,48},{64,56},{72,6... | collective-permute-start | bytes 6152 | tf_op jit(solution)/shard_map/ppermute | solution.py:14
  323.4 8.8 %collective-permute-start.7 = (f32[512]{0:T(512)S(1)}, f32[512]{0:T(512)S(1)}, u32[]{:S(2)}, u32[]{:S(2)}) collective-permute-start(f32[512]{0:T(512)S(1)} %multiply_add_fusion.33), channel_id=1, source_target_pairs={{8,0},{16,8},{24,16},{32,24},{40,32},{48,40},{56,48},{64,56},{72,6... | collective-permute-start | bytes 6152 | tf_op jit(solution)/shard_map/ppermute | solution.py:14
  332.2 8.8 %collective-permute-start.8 = (f32[512]{0:T(512)S(1)}, f32[512]{0:T(512)S(1)}, u32[]{:S(2)}, u32[]{:S(2)}) collective-permute-start(f32[512]{0:T(512)S(1)} %multiply_add_fusion.32), channel_id=1, source_target_pairs={{8,0},{16,8},{24,16},{32,24},{40,32},{48,40},{56,48},{64,56},{72,6... | collective-permute-start | bytes 6152 | tf_op jit(solution)/shard_map/ppermute | solution.py:14
  341.0 8.8 %collective-permute-start.9 = (f32[512]{0:T(512)S(1)}, f32[512]{0:T(512)S(1)}, u32[]{:S(2)}, u32[]{:S(2)}) collective-permute-start(f32[512]{0:T(512)S(1)} %multiply_add_fusion.31), channel_id=1, source_target_pairs={{8,0},{16,8},{24,16},{32,24},{40,32},{48,40},{56,48},{64,56},{72,6... | collective-permute-start | bytes 6152 | tf_op jit(solution)/shard_map/ppermute | solution.py:14
  349.8 8.8 %collective-permute-start.10 = (f32[512]{0:T(512)S(1)}, f32[512]{0:T(512)S(1)}, u32[]{:S(2)}, u32[]{:S(2)}) collective-permute-start(f32[512]{0:T(512)S(1)} %multiply_add_fusion.30), channel_id=1, source_target_pairs={{8,0},{16,8},{24,16},{32,24},{40,32},{48,40},{56,48},{64,56},{72,6... | collective-permute-start | bytes 6152 | tf_op jit(solution)/shard_map/ppermute | solution.py:14
  358.5 8.8 %collective-permute-start.11 = (f32[512]{0:T(512)S(1)}, f32[512]{0:T(512)S(1)}, u32[]{:S(2)}, u32[]{:S(2)}) collective-permute-start(f32[512]{0:T(512)S(1)} %multiply_add_fusion.29), channel_id=1, source_target_pairs={{8,0},{16,8},{24,16},{32,24},{40,32},{48,40},{56,48},{64,56},{72,6... | collective-permute-start | bytes 6152 | tf_op jit(solution)/shard_map/ppermute | solution.py:14
  367.3 8.8 %collective-permute-start.12 = (f32[512]{0:T(512)S(1)}, f32[512]{0:T(512)S(1)}, u32[]{:S(2)}, u32[]{:S(2)}) collective-permute-start(f32[512]{0:T(512)S(1)} %multiply_add_fusion.28), channel_id=1, source_target_pairs={{8,0},{16,8},{24,16},{32,24},{40,32},{48,40},{56,48},{64,56},{72,6... | collective-permute-start | bytes 6152 | tf_op jit(solution)/shard_map/ppermute | solution.py:14
  376.1 8.8 %collective-permute-start.13 = (f32[512]{0:T(512)S(1)}, f32[512]{0:T(512)S(1)}, u32[]{:S(2)}, u32[]{:S(2)}) collective-permute-start(f32[512]{0:T(512)S(1)} %multiply_add_fusion.27), channel_id=1, source_target_pairs={{8,0},{16,8},{24,16},{32,24},{40,32},{48,40},{56,48},{64,56},{72,6... | collective-permute-start | bytes 6152 | tf_op jit(solution)/shard_map/ppermute | solution.py:14
  384.9 8.8 %collective-permute-start.14 = (f32[512]{0:T(512)S(1)}, f32[512]{0:T(512)S(1)}, u32[]{:S(2)}, u32[]{:S(2)}) collective-permute-start(f32[512]{0:T(512)S(1)} %multiply_add_fusion.26), channel_id=1, source_target_pairs={{8,0},{16,8},{24,16},{32,24},{40,32},{48,40},{56,48},{64,56},{72,6... | collective-permute-start | bytes 6152 | tf_op jit(solution)/shard_map/ppermute | solution.py:14
  393.7 8.8 %collective-permute-start.15 = (f32[512]{0:T(512)S(1)}, f32[512]{0:T(512)S(1)}, u32[]{:S(2)}, u32[]{:S(2)}) collective-permute-start(f32[512]{0:T(512)S(1)} %multiply_add_fusion.25), channel_id=1, source_target_pairs={{8,0},{16,8},{24,16},{32,24},{40,32},{48,40},{56,48},{64,56},{72,6... | collective-permute-start | bytes 6152 | tf_op jit(solution)/shard_map/ppermute | solution.py:14
  402.5 8.8 %collective-permute-start.16 = (f32[512]{0:T(512)S(1)}, f32[512]{0:T(512)S(1)}, u32[]{:S(2)}, u32[]{:S(2)}) collective-permute-start(f32[512]{0:T(512)S(1)} %multiply_add_fusion.24), channel_id=1, source_target_pairs={{8,0},{16,8},{24,16},{32,24},{40,32},{48,40},{56,48},{64,56},{72,6... | collective-permute-start | bytes 6152 | tf_op jit(solution)/shard_map/ppermute | solution.py:14
  411.3 8.8 %collective-permute-start.17 = (f32[512]{0:T(512)S(1)}, f32[512]{0:T(512)S(1)}, u32[]{:S(2)}, u32[]{:S(2)}) collective-permute-start(f32[512]{0:T(512)S(1)} %multiply_add_fusion.23), channel_id=1, source_target_pairs={{8,0},{16,8},{24,16},{32,24},{40,32},{48,40},{56,48},{64,56},{72,6... | collective-permute-start | bytes 6152 | tf_op jit(solution)/shard_map/ppermute | solution.py:14
  420.1 8.8 %collective-permute-start.18 = (f32[512]{0:T(512)S(1)}, f32[512]{0:T(512)S(1)}, u32[]{:S(2)}, u32[]{:S(2)}) collective-permute-start(f32[512]{0:T(512)S(1)} %multiply_add_fusion.22), channel_id=1, source_target_pairs={{8,0},{16,8},{24,16},{32,24},{40,32},{48,40},{56,48},{64,56},{72,6... | collective-permute-start | bytes 6152 | tf_op jit(solution)/shard_map/ppermute | solution.py:14
  428.9 8.8 %collective-permute-start.19 = (f32[512]{0:T(512)S(1)}, f32[512]{0:T(512)S(1)}, u32[]{:S(2)}, u32[]{:S(2)}) collective-permute-start(f32[512]{0:T(512)S(1)} %multiply_add_fusion.21), channel_id=1, source_target_pairs={{8,0},{16,8},{24,16},{32,24},{40,32},{48,40},{56,48},{64,56},{72,6... | collective-permute-start | bytes 6152 | tf_op jit(solution)/shard_map/ppermute | solution.py:14
  437.7 8.8 %collective-permute-start.20 = (f32[512]{0:T(512)S(1)}, f32[512]{0:T(512)S(1)}, u32[]{:S(2)}, u32[]{:S(2)}) collective-permute-start(f32[512]{0:T(512)S(1)} %multiply_add_fusion.20), channel_id=1, source_target_pairs={{8,0},{16,8},{24,16},{32,24},{40,32},{48,40},{56,48},{64,56},{72,6... | collective-permute-start | bytes 6152 | tf_op jit(solution)/shard_map/ppermute | solution.py:14
  446.5 8.8 %collective-permute-start.21 = (f32[512]{0:T(512)S(1)}, f32[512]{0:T(512)S(1)}, u32[]{:S(2)}, u32[]{:S(2)}) collective-permute-start(f32[512]{0:T(512)S(1)} %multiply_add_fusion.19), channel_id=1, source_target_pairs={{8,0},{16,8},{24,16},{32,24},{40,32},{48,40},{56,48},{64,56},{72,6... | collective-permute-start | bytes 6152 | tf_op jit(solution)/shard_map/ppermute | solution.py:14
  455.3 8.8 %collective-permute-start.22 = (f32[512]{0:T(512)S(1)}, f32[512]{0:T(512)S(1)}, u32[]{:S(2)}, u32[]{:S(2)}) collective-permute-start(f32[512]{0:T(512)S(1)} %multiply_add_fusion.18), channel_id=1, source_target_pairs={{8,0},{16,8},{24,16},{32,24},{40,32},{48,40},{56,48},{64,56},{72,6... | collective-permute-start | bytes 6152 | tf_op jit(solution)/shard_map/ppermute | solution.py:14
  464.1 8.8 %collective-permute-start.23 = (f32[512]{0:T(512)S(1)}, f32[512]{0:T(512)S(1)}, u32[]{:S(2)}, u32[]{:S(2)}) collective-permute-start(f32[512]{0:T(512)S(1)} %multiply_add_fusion.17), channel_id=1, source_target_pairs={{8,0},{16,8},{24,16},{32,24},{40,32},{48,40},{56,48},{64,56},{72,6... | collective-permute-start | bytes 6152 | tf_op jit(solution)/shard_map/ppermute | solution.py:14
  472.8 8.8 %collective-permute-start.24 = (f32[512]{0:T(512)S(1)}, f32[512]{0:T(512)S(1)}, u32[]{:S(2)}, u32[]{:S(2)}) collective-permute-start(f32[512]{0:T(512)S(1)} %multiply_add_fusion.16), channel_id=1, source_target_pairs={{8,0},{16,8},{24,16},{32,24},{40,32},{48,40},{56,48},{64,56},{72,6... | collective-permute-start | bytes 6152 | tf_op jit(solution)/shard_map/ppermute | solution.py:14
  481.6 8.8 %collective-permute-start.25 = (f32[512]{0:T(512)S(1)}, f32[512]{0:T(512)S(1)}, u32[]{:S(2)}, u32[]{:S(2)}) collective-permute-start(f32[512]{0:T(512)S(1)} %multiply_add_fusion.15), channel_id=1, source_target_pairs={{8,0},{16,8},{24,16},{32,24},{40,32},{48,40},{56,48},{64,56},{72,6... | collective-permute-start | bytes 6152 | tf_op jit(solution)/shard_map/ppermute | solution.py:14
  490.4 8.8 %collective-permute-start.26 = (f32[512]{0:T(512)S(1)}, f32[512]{0:T(512)S(1)}, u32[]{:S(2)}, u32[]{:S(2)}) collective-permute-start(f32[512]{0:T(512)S(1)} %multiply_add_fusion.14), channel_id=1, source_target_pairs={{8,0},{16,8},{24,16},{32,24},{40,32},{48,40},{56,48},{64,56},{72,6... | collective-permute-start | bytes 6152 | tf_op jit(solution)/shard_map/ppermute | solution.py:14
  499.2 8.8 %collective-permute-start.27 = (f32[512]{0:T(512)S(1)}, f32[512]{0:T(512)S(1)}, u32[]{:S(2)}, u32[]{:S(2)}) collective-permute-start(f32[512]{0:T(512)S(1)} %multiply_add_fusion.13), channel_id=1, source_target_pairs={{8,0},{16,8},{24,16},{32,24},{40,32},{48,40},{56,48},{64,56},{72,6... | collective-permute-start | bytes 6152 | tf_op jit(solution)/shard_map/ppermute | solution.py:14
  508.0 8.8 %collective-permute-start.28 = (f32[512]{0:T(512)S(1)}, f32[512]{0:T(512)S(1)}, u32[]{:S(2)}, u32[]{:S(2)}) collective-permute-start(f32[512]{0:T(512)S(1)} %multiply_add_fusion.12), channel_id=1, source_target_pairs={{8,0},{16,8},{24,16},{32,24},{40,32},{48,40},{56,48},{64,56},{72,6... | collective-permute-start | bytes 6152 | tf_op jit(solution)/shard_map/ppermute | solution.py:14
  516.8 8.8 %collective-permute-start.29 = (f32[512]{0:T(512)S(1)}, f32[512]{0:T(512)S(1)}, u32[]{:S(2)}, u32[]{:S(2)}) collective-permute-start(f32[512]{0:T(512)S(1)} %multiply_add_fusion.11), channel_id=1, source_target_pairs={{8,0},{16,8},{24,16},{32,24},{40,32},{48,40},{56,48},{64,56},{72,6... | collective-permute-start | bytes 6152 | tf_op jit(solution)/shard_map/ppermute | solution.py:14
  525.6 23.2 %collective-permute-start.30 = (f32[512]{0:T(512)S(1)}, f32[512]{0:T(512)S(1)}, u32[]{:S(2)}, u32[]{:S(2)}) collective-permute-start(f32[512]{0:T(512)S(1)} %multiply_add_fusion.10), channel_id=1, source_target_pairs={{8,0},{16,8},{24,16},{32,24},{40,32},{48,40},{56,48},{64,56},{72,6... | collective-permute-start | bytes 6152 | tf_op jit(solution)/shard_map/ppermute | solution.py:14
  534.9 16.3 %copy-start.1 = (bf16[512,512]{1,0:T(8,128)(2,1)S(1)}, bf16[512,512]{1,0:T(8,128)(2,1)}, u32[]{:S(2)}) copy-start(bf16[512,512]{1,0:T(8,128)(2,1)} %param.7) | copy-start | bytes 1572868
Sparse Core Ops, SparseCore 0:
  161.9 69.3 all-reduce.37
